TPU v7x, 256 devices: a whole 4x4x8 slice. The times are simulated.
256 devices in a mesh: ctx: 16 (over z_lo, y, core), heads: 16 (over z_hi, x).
Axes of the slice: x: 4, y: 4, z: 8 (z_hi: 4, z_lo: 2; z = z_hi * 2 + z_lo), core: 2. Of those that a mesh axis runs over, the one named last changes fastest.
Arguments:
- queries: bfloat16 [4096, 8192], P('ctx', 'heads'), may hold values from -48 to 48
- out_grad: bfloat16 [4096, 8192], P('ctx', 'heads'), may hold values from -48 to 48
- attn_out: bfloat16 [4096, 8192], P('ctx', 'heads'), may hold values from -6 to 6
- img_keys: bfloat16 [2048, 1024], P('ctx'), may hold values from -6 to 6
- img_values: bfloat16 [2048, 1024], P('ctx'), may hold values from -6 to 6
- key_weight: bfloat16 [8192, 1024], P('heads'), may hold values from -0.0625 to 0.0625
- value_weight: bfloat16 [8192, 1024], P('heads'), may hold values from -0.0625 to 0.0625
- proj_weight: bfloat16 [7680, 8192], P('heads'), may hold values from -0.0625 to 0.0625
- block_order: int32 [32], replicated, may hold values from 0 to 31, each once
- owner_counts: int32 [16], replicated, may hold values from 1 to 4, 32 in all
Outputs:
- d_query: bfloat16 [4096, 8192], P('ctx', 'heads')
- d_vision: bfloat16 [4096, 7680], P('ctx', 'heads')
Inputs may be any that keep to these rules, and one draw needn't show every extreme that they name: `block_order`: each of the 32 blocks appears once. `owner_counts`: the counts sum to 32; one owner has exactly 4.
All inputs are finite; a program needn't handle non-finite values.
Results may differ from a plain program's by a relative error of at most 0.015.
Values may be sent and summed in bfloat16 or wider, within the bound.
No kernel may reach another device: no remote copies, remote signals or barrier semaphores. Data moves between devices by JAX's collectives and lax.ppermute only.
A program may use at most 64 MiB of HBM per device.

v0:
```python
import jax
import jax.numpy as jnp
from jax import lax
from jax.sharding import PartitionSpec as P

KVH = 8
HD = 128
BR = 64
CAP = 4
CONTRACT_LAST = (((1,), (1,)), ((), ()))
CONTRACT_FIRST = (((0,), (0,)), ((), ()))


def from_everyone(array, axis):
    copies = jnp.broadcast_to(array, (lax.axis_size(axis), *array.shape))
    return lax.all_to_all(copies, axis, split_axis=0, concat_axis=0, tiled=True)


def laid_out(pieces, dim):
    shape = list(pieces.shape[1:])
    shape[dim] *= pieces.shape[0]
    return jnp.moveaxis(pieces, 0, dim).reshape(shape)


def gathered_copies(array, axis, dim):
    pieces = from_everyone(array, axis)
    return laid_out(pieces, dim)


def in_one_piece(arrays, axis, dim, along):
    both = jnp.concatenate(arrays, axis=along)
    filled, at, outs = (gathered_copies(both, axis, dim), 0, [])
    for a in arrays:
        outs.append(lax.slice_in_dim(filled, at, at + a.shape[along], axis=along))
        at += a.shape[along]
    return tuple(outs)


def split_up(array, dim, peers):
    shape = array.shape
    pieces = array.reshape(*shape[:dim], peers, shape[dim] // peers, *shape[dim + 1 :])
    return jnp.moveaxis(pieces, dim, 0)


def sum_at_owner(array, axis, dim):
    peers = lax.axis_size(axis)
    pieces = lax.all_to_all(split_up(array, dim, peers), axis, 0, 0, tiled=True)
    return jnp.sum(pieces, axis=0)


def owner_table(block_order, owner_counts, capacity):
    offsets = jnp.cumsum(owner_counts) - owner_counts
    columns = jnp.arange(capacity, dtype=jnp.int32)
    position = offsets[:, None] + columns[None, :]
    living = columns[None, :] < owner_counts[:, None]
    blocks = jnp.arange(block_order.shape[0], dtype=jnp.int32)
    matches = position[:, :, None] == blocks[None, None, :]
    chosen = jnp.sum(jnp.where(matches, block_order[None, None, :], 0), axis=2)
    return (jnp.where(living, chosen, 0), living)


def image_section(grad_rows, key_weight, value_weight, proj_weight):
    row_count = grad_rows.shape[0]
    group_devices = lax.axis_size("heads") // KVH
    pieces = lax.all_gather(grad_rows.astype(jnp.bfloat16), "heads", axis=1, tiled=True).astype(
        grad_rows.dtype
    )
    pieces = jnp.sum(pieces.reshape(row_count, KVH, group_devices, 2, HD), axis=2).astype(
        jnp.bfloat16
    )
    key_grads = pieces[:, :, 0].reshape(row_count, KVH * HD)
    value_grads = pieces[:, :, 1].reshape(row_count, KVH * HD)
    image_part = lax.dot_general(
        key_grads, key_weight, CONTRACT_LAST, preferred_element_type=jnp.float32
    )
    image_part = image_part + lax.dot_general(
        value_grads, value_weight, CONTRACT_LAST, preferred_element_type=jnp.float32
    )
    image_part = image_part.astype(jnp.bfloat16)
    vision = lax.dot_general(
        lax.all_gather(image_part, "heads", axis=1, tiled=True),
        proj_weight,
        CONTRACT_LAST,
        preferred_element_type=jnp.float32,
    )
    return vision.astype(jnp.bfloat16)


def shards(
    queries,
    out_grad,
    attn_out,
    img_keys,
    img_values,
    key_weight,
    value_weight,
    proj_weight,
    block_order,
    owner_counts,
):
    scaling = HD ** (-0.5)
    text_rows = queries.shape[0]
    local_heads = queries.shape[1] // HD
    group_devices = lax.axis_size("heads") // KVH
    group_index = lax.axis_index("heads") // group_devices
    kv_column = group_index * HD
    own_keys = lax.dynamic_slice_in_dim(img_keys, kv_column, HD, 1)
    own_values = lax.dynamic_slice_in_dim(img_values, kv_column, HD, 1)
    keys_all, values_all = in_one_piece((own_keys, own_values), "ctx", 0, 1)
    query_rows = queries.reshape(text_rows * local_heads, HD)
    grad_rows = out_grad.reshape(text_rows * local_heads, HD)
    output_rows = attn_out.reshape(text_rows * local_heads, HD)
    scores = (
        lax.dot_general(query_rows, keys_all, CONTRACT_LAST, preferred_element_type=jnp.float32)
        * scaling
    )
    weights = jnp.exp(scores - jax.nn.logsumexp(scores, axis=1, keepdims=True))
    weights_low = weights.astype(jnp.bfloat16)
    dweights = lax.dot_general(
        grad_rows, values_all, CONTRACT_LAST, preferred_element_type=jnp.float32
    )
    delta = jnp.sum(
        grad_rows.astype(jnp.float32) * output_rows.astype(jnp.float32), axis=1, keepdims=True
    )
    dscores = (weights * (dweights - delta)).astype(jnp.bfloat16)
    grad_query = jnp.dot(dscores, keys_all, preferred_element_type=jnp.float32) * scaling
    d_query = grad_query.astype(jnp.bfloat16).reshape(text_rows, local_heads * HD)
    ctx_count = lax.axis_size("ctx")
    ctx_index = lax.axis_index("ctx")
    block_total = block_order.shape[0]
    local_count = block_total // ctx_count
    slots, living = owner_table(block_order, owner_counts, CAP)
    my_slots = lax.dynamic_index_in_dim(slots, ctx_index, 0, keepdims=False)
    my_living = lax.dynamic_index_in_dim(living, ctx_index, 0, keepdims=False)
    grad_key = (
        lax.dot_general(dscores, query_rows, CONTRACT_FIRST, preferred_element_type=jnp.float32)
        * scaling
    )
    grad_value = lax.dot_general(
        weights_low, grad_rows, CONTRACT_FIRST, preferred_element_type=jnp.float32
    )
    shared = sum_at_owner(jnp.concatenate([grad_key, grad_value], axis=1), "ctx", 0)
    vision = image_section(shared, key_weight, value_weight, proj_weight)
    width_here = vision.shape[1]
    blocks = jnp.arange(block_total, dtype=jnp.int32)
    owned = jnp.any((slots[:, :, None] == blocks[None, None, :]) & living[:, :, None], axis=1)
    selected = lax.dynamic_slice_in_dim(owned, ctx_index * local_count, local_count, 1)
    local_blocks = vision.reshape(1, local_count, BR, width_here)
    outgoing = jnp.where(selected[:, :, None, None], local_blocks, jnp.zeros((), jnp.bfloat16))
    arrived = lax.all_to_all(outgoing, "ctx", split_axis=0, concat_axis=0, tiled=True)
    arrived = arrived.reshape(block_total, BR, width_here)
    picked = jnp.take(arrived, my_slots, axis=0)
    picked = jnp.where(my_living[:, None, None], picked, jnp.zeros_like(picked))
    d_vision = picked.reshape(CAP * BR, picked.shape[2])
    return (d_query, d_vision)


def solution(mesh):
    placed = (
        P("ctx", "heads"),
        P("ctx", "heads"),
        P("ctx", "heads"),
        P("ctx", None),
        P("ctx", None),
        P("heads", None),
        P("heads", None),
        P("heads", None),
        P(),
        P(),
    )
    return jax.shard_map(
        shards,
        mesh=mesh,
        in_specs=placed,
        out_specs=(P("ctx", "heads"), P("ctx", "heads")),
        check_vma=False,
    )
```

profile of v0, /device:TPU:25, one launch (start us, length us, event | category | flops | bytes accessed | tf_op | source)
XLA Modules:
  0.0 243.8 jit_solution(9903565578479135084)
XLA Ops:
  7.2 0.9 constant_dynamic-slice_fusion.1
  8.1 1.1 broadcast_in_dim.90
  9.2 6.4 %all-to-all-start = ((bf16[16,128,256]{2,1,0:T(8,128)(2,1)}), bf16[16,128,256]{2,1,0:T(8,128)(2,1)S(1)}, u32[]{:S(2)}, u32[]{:S(2)}) async-start(bf16[16,128,256]{2,1,0:T(8,128)(2,1)} %broadcast_in_dim.90), calls=%async_computation | async-start | bytes 2097152 | tf_op jit(solution)/shard_map/all_to_all | solution.py:16
  15.6 1.1 reshape.180
  16.7 1.1 reshape.181
  17.8 1.1 reshape.189
  18.9 0.2 multiply_reduce_fusion.1
  19.1 11.5 %all-to-all-done = bf16[16,128,256]{2,1,0:T(8,128)(2,1)S(1)} async-done(((bf16[16,128,256]{2,1,0:T(8,128)(2,1)}), bf16[16,128,256]{2,1,0:T(8,128)(2,1)S(1)}, u32[]{:S(2)}, u32[]{:S(2)}) %all-to-all-start) | async-done | bytes 1048608 | tf_op jit(solution)/shard_map/all_to_all | solution.py:16
  30.6 1.3 multiply_reduce_fusion
  31.9 1.4 exponential_reduce_fusion
  33.3 1.7 fusion.1
  35.0 2.1 multiply_convert_fusion
  37.2 1.9 copy-done.1
  39.1 1.5 convolution_multiply_fusion
  40.7 0.2 copy_bitcast_fusion
  40.9 29.9 %all_to_all.15 = f32[16,128,256]{1,2,0:T(8,128)S(1)} all-to-all(f32[16,128,256]{1,2,0:T(8,128)S(1)} %copy_bitcast_fusion), channel_id=1, replica_groups=mesh['ctx'=16,'heads'=16] {'ctx'}, dimensions={0} | all-to-all | bytes 4194304 | tf_op jit(solution)/shard_map/all_to_all | solution.py:47
  70.8 0.7 reduce_sum.48
  71.6 53.2 %all-gather.3.cloned.1.call-done = bf16[128,4096]{0,1:T(8,128)(2,1)} async-done(((bf16[128,256]{0,1:T(8,128)(2,1)}), bf16[128,4096]{0,1:T(8,128)(2,1)}) %all-gather.3.cloned.1.call-update) | async-done | bytes 1048592 | tf_op jit(solution)/shard_map/all_gather | solution.py:65
  124.8 1.5 reduce.2
  126.3 0.5 fusion.17
  126.8 2.4 fusion.6
  129.5 0.2 select_reduce_fusion
  129.9 60.9 %all-gather.5.cloned.1.call-done = bf16[128,8192]{1,0:T(8,128)(2,1)} async-done(((bf16[128,512]{1,0:T(8,128)(2,1)}), bf16[128,8192]{1,0:T(8,128)(2,1)}) %all-gather.5.cloned.1.call-update) | async-done | bytes 2097168 | tf_op jit(solution)/shard_map/all_gather | solution.py:81
  190.9 6.1 %convolution_convert_fusion = bf16[128,480]{0,1:T(8,128)(2,1)S(1)} fusion(bf16[128,8192]{1,0:T(8,128)(2,1)} %all-gather.5.cloned.1.call-done, bf16[480,8192]{1,0:T(8,128)(2,1)} %param.17), kind=kOutput, calls=%fused_computation.17 | convolution fusion | flops 1006694400 | bytes 10084352 | tf_op jit(solution)/shard_map/dot_general | solution.py:80
  197.0 1.6 broadcast_select_fusion
  198.6 5.6 %all-to-all-start.2 = ((bf16[16,2,64,480]{3,2,1,0:T(8,128)(2,1)}), bf16[16,2,64,480]{3,2,1,0:T(8,128)(2,1)}, u32[]{:S(2)}, u32[]{:S(2)}) async-start(bf16[16,2,64,480]{3,2,1,0:T(8,128)(2,1)} %broadcast_select_fusion), calls=%async_computation.2 | async-start | bytes 4194304 | tf_op jit(solution)/shard_map/all_to_all | solution.py:150
  204.4 0.2 dynamic-slice_reduce_fusion.1
  204.9 3.5 %fusion.5 = bf16[1024,128]{1,0:T(8,128)(2,1)S(1)} fusion(bf16[2048,1024]{1,0:T(8,128)(2,1)} %copy-done.1, bf16[2048,256]{1,0:T(8,128)(2,1)S(1)} %bitcast.34), kind=kOutput, calls=%fused_computation.14 | convolution fusion | flops 537133056 | bytes 4980736 | tf_op jit(solution)/shard_map/dot_general | solution.py:126
  208.4 0.9 reshape.182
  209.3 24.5 %all-to-all-done.2 = bf16[16,2,64,480]{3,2,1,0:T(8,128)(2,1)} async-done(((bf16[16,2,64,480]{3,2,1,0:T(8,128)(2,1)}), bf16[16,2,64,480]{3,2,1,0:T(8,128)(2,1)}, u32[]{:S(2)}, u32[]{:S(2)}) %all-to-all-start.2) | async-done | bytes 1966112 | tf_op jit(solution)/shard_map/all_to_all | solution.py:150
  233.8 2.2 gather_fusion
  236.1 0.8 copy.36
  (38 shorter events, 1.4 us)
Async XLA Ops:
  7.2 119.2 %copy-start = (bf16[512,1024]{1,0:T(8,128)(2,1)S(1)}, bf16[512,1024]{1,0:T(8,128)(2,1)}, u32[]{:S(2)}) copy-start(bf16[512,1024]{1,0:T(8,128)(2,1)} %param.15) | copy-start | bytes 3145732
  9.2 21.4 %all-to-all-start = ((bf16[16,128,256]{2,1,0:T(8,128)(2,1)}), bf16[16,128,256]{2,1,0:T(8,128)(2,1)S(1)}, u32[]{:S(2)}, u32[]{:S(2)}) async-start(bf16[16,128,256]{2,1,0:T(8,128)(2,1)} %broadcast_in_dim.90), calls=%async_computation | async-start | bytes 2097152 | tf_op jit(solution)/shard_map/all_to_all | solution.py:16
  15.5 109.3 %all-gather.3.cloned.1.call-start = ((), (), s32[]{:S(2)}) async-start(), calls=%async_computation.3 | async-start | bytes 1114112 | tf_op jit(solution)/shard_map/all_gather | solution.py:65
  30.6 4.4 %copy-start.2 = (bf16[16,128,256]{2,1,0:T(8,128)(2,1)}, bf16[16,128,256]{2,1,0:T(8,128)(2,1)S(1)}, u32[]{:S(2)}) copy-start(bf16[16,128,256]{2,1,0:T(8,128)(2,1)S(1)} %all-to-all-done) | copy-start | bytes 3145732
  37.2 1.9 copy-start.1
  40.7 88.6 %copy-start.4 = (s32[16]{0:T(128)S(1)}, s32[16]{0:T(128)}, u32[]{:S(2)}) copy-start(s32[16]{0:T(128)} %param.19) | copy-start | bytes 196
  40.7 88.8 %copy-start.5 = (s32[32]{0:T(128)S(1)}, s32[32]{0:T(128)}, u32[]{:S(2)}) copy-start(s32[32]{0:T(128)} %param.18) | copy-start | bytes 388
  71.5 119.3 %all-gather.5.cloned.1.call-start = ((), (), s32[]{:S(2)}) async-start(), calls=%async_computation.4 | async-start | bytes 2228224 | tf_op jit(solution)/shard_map/all_gather | solution.py:81
  129.9 75.0 %copy-start.3 = (bf16[16,128,256]{2,1,0:T(8,128)(2,1)S(1)}, bf16[16,128,256]{2,1,0:T(8,128)(2,1)}, u32[]{:S(2)}) copy-start(bf16[16,128,256]{2,1,0:T(8,128)(2,1)} %copy-done.2) | copy-start | bytes 3145732
  198.6 35.2 %all-to-all-start.2 = ((bf16[16,2,64,480]{3,2,1,0:T(8,128)(2,1)}), bf16[16,2,64,480]{3,2,1,0:T(8,128)(2,1)}, u32[]{:S(2)}, u32[]{:S(2)}) async-start(bf16[16,2,64,480]{3,2,1,0:T(8,128)(2,1)} %broadcast_select_fusion), calls=%async_computation.2 | async-start | bytes 4194304 | tf_op jit(solution)/shard_map/all_to_all | solution.py:150
Sparse Core Ops, SparseCore 0:
  71.6 53.1 all-gather.2
  129.4 61.4 all-gather.4
where the time goes:
time: 244 us
  waiting for transfers between devices  150 us (61%)
  blocking collectives  29.9 us (12%)
  matrix products  19 us (8%)
  between operations  14.3 us (6%)
  local copies, waits for them, and re-layouts  12.1 us (5%)
  starting transfers between devices  12 us (5%)
  other arithmetic  6.27 us (3%)
    all_gather x1, waiting for transfers between devices, image_section(): lax.all_gather(image_part, 'heads', axis=1, tiled=True)  60.9 us
    all_gather x1, waiting for transfers between devices, image_section(): lax.all_gather(grad_rows.astype(jnp.bfloat16), 'heads', axis=1, tiled=True)  53.2 us
    all_to_all x1, blocking collectives, sum_at_owner(): pieces = lax.all_to_all(split_up(array, dim, peers), axis, 0, 0, tiled=True)  29.9 us
    all_to_all x1, waiting for transfers between devices, shards(): lax.all_to_all(outgoing, 'ctx', split_axis=0, concat_axis=0, tiled=True)  24.5 us
    all_to_all x1, waiting for transfers between devices, from_everyone(): return lax.all_to_all(copies, axis, split_axis=0, concat_axis=0, tiled=True)  11.5 us
    all_to_all x1, starting transfers between devices, from_everyone(): return lax.all_to_all(copies, axis, split_axis=0, concat_axis=0, tiled=True)  6.37 us
    dot_general x1, matrix products, image_section(): lax.dot_general(lax.all_gather(image_part, 'heads', axis=1, tiled=True),...  6.06 us
    all_to_all x1, starting transfers between devices, shards(): lax.all_to_all(outgoing, 'ctx', split_axis=0, concat_axis=0, tiled=True)  5.58 us
  transfers between devices with their start and end apart: 4, of which 4 were waited for; matrix products, arithmetic and copies ran while one was open for 4% of the time, Pallas kernels for 0%

commit v1 on v0

--- a/solution.py
+++ b/solution.py
@@ -62,9 +62,12 @@
 def image_section(grad_rows, key_weight, value_weight, proj_weight):
     row_count = grad_rows.shape[0]
     group_devices = lax.axis_size("heads") // KVH
-    pieces = lax.all_gather(grad_rows.astype(jnp.bfloat16), "heads", axis=1, tiled=True).astype(
-        grad_rows.dtype
-    )
+    pieces = jnp.concatenate(
+        lax.all_to_all(
+            jnp.stack([grad_rows.astype(jnp.bfloat16)] * lax.axis_size("heads")), "heads", 0, 0
+        ),
+        axis=1,
+    ).astype(grad_rows.dtype)
     pieces = jnp.sum(pieces.reshape(row_count, KVH, group_devices, 2, HD), axis=2).astype(
         jnp.bfloat16
     )

time: 244 us -> 226 us (0.926)
  waiting for transfers between devices: 150 us -> 95.5 us
  blocking collectives: 29.9 us -> 67.6 us
    all_gather x1 -> x0, waiting for transfers between devices: 53.2 us -> none  [image_section(): lax.all_gather(grad_rows.astype(jnp.bfloat16), 'heads', axis=1, tiled=True)]
    all_to_all x0 -> x1, blocking collectives: none -> 37.7 us  [image_section(): lax.all_to_all(jnp.stack([grad_rows.astype(jnp.bfloat16)] * lax.axis_size...]
  transfers between devices with their start and end apart: 4 -> 3, of which waited for: 4 -> 3; matrix products, arithmetic and copies ran while one was open for 4% -> 4% of each run, Pallas kernels for 0% -> 0%
where the time goes in v1:
time: 226 us; the launch traced here: 225 us
  waiting for transfers between devices  95.5 us (42%)
  blocking collectives  67.6 us (30%)
  matrix products  19 us (8%)
  between operations  14.3 us (6%)
  local copies, waits for them, and re-layouts  12.3 us (5%)
  starting transfers between devices  12 us (5%)
  other arithmetic  4.43 us (2%)
    all_gather x1, waiting for transfers between devices, image_section(): lax.all_gather(image_part, 'heads', axis=1, tiled=True)  59.5 us
    all_to_all x1, blocking collectives, image_section(): lax.all_to_all(jnp.stack([grad_rows.astype(jnp.bfloat16)] * lax.axis_size...  37.7 us
    all_to_all x1, blocking collectives, sum_at_owner(): pieces = lax.all_to_all(split_up(array, dim, peers), axis, 0, 0, tiled=True)  29.9 us
    all_to_all x1, waiting for transfers between devices, shards(): lax.all_to_all(outgoing, 'ctx', split_axis=0, concat_axis=0, tiled=True)  24.5 us
    all_to_all x1, waiting for transfers between devices, from_everyone(): return lax.all_to_all(copies, axis, split_axis=0, concat_axis=0, tiled=True)  11.5 us
    all_to_all x1, starting transfers between devices, from_everyone(): return lax.all_to_all(copies, axis, split_axis=0, concat_axis=0, tiled=True)  6.37 us
    dot_general x1, matrix products, image_section(): lax.dot_general(lax.all_gather(image_part, 'heads', axis=1, tiled=True),...  6.07 us
    all_to_all x1, starting transfers between devices, shards(): lax.all_to_all(outgoing, 'ctx', split_axis=0, concat_axis=0, tiled=True)  5.58 us
  transfers between devices with their start and end apart: 3, of which 3 were waited for; matrix products, arithmetic and copies ran while one was open for 4% of the time, Pallas kernels for 0%

profile of v1, /device:TPU:25, one launch (start us, length us, event | category | flops | bytes accessed | tf_op | source)
XLA Modules:
  0.0 225.1 jit_solution(2334528711314793425)
XLA Ops:
  7.2 0.9 constant_dynamic-slice_fusion.1
  8.1 1.1 broadcast_in_dim.90
  9.2 6.4 %all-to-all-start = ((bf16[16,128,256]{2,1,0:T(8,128)(2,1)}), bf16[16,128,256]{2,1,0:T(8,128)(2,1)S(1)}, u32[]{:S(2)}, u32[]{:S(2)}) async-start(bf16[16,128,256]{2,1,0:T(8,128)(2,1)} %broadcast_in_dim.90), calls=%async_computation | async-start | bytes 2097152 | tf_op jit(solution)/shard_map/all_to_all | solution.py:16
  15.6 1.1 reshape.184
  16.7 1.1 reshape.185
  17.8 1.1 reshape.193
  18.9 0.2 multiply_reduce_fusion.1
  19.1 11.5 %all-to-all-done = bf16[16,128,256]{2,1,0:T(8,128)(2,1)S(1)} async-done(((bf16[16,128,256]{2,1,0:T(8,128)(2,1)}), bf16[16,128,256]{2,1,0:T(8,128)(2,1)S(1)}, u32[]{:S(2)}, u32[]{:S(2)}) %all-to-all-start) | async-done | bytes 1048608 | tf_op jit(solution)/shard_map/all_to_all | solution.py:16
  30.6 1.3 multiply_reduce_fusion
  31.9 1.4 exponential_reduce_fusion
  33.3 1.7 fusion.1
  35.0 2.1 multiply_convert_fusion
  37.2 1.9 copy-done.1
  39.1 1.5 convolution_multiply_fusion
  40.7 0.2 copy_bitcast_fusion
  40.9 29.9 %all_to_all.20 = f32[16,128,256]{1,2,0:T(8,128)S(1)} all-to-all(f32[16,128,256]{1,2,0:T(8,128)S(1)} %copy_bitcast_fusion), channel_id=1, replica_groups=mesh['ctx'=16,'heads'=16] {'ctx'}, dimensions={0} | all-to-all | bytes 4194304 | tf_op jit(solution)/shard_map/all_to_all | solution.py:47
  70.9 0.2 stack.2
  71.1 37.7 %all_to_all.21 = bf16[16,128,256]{1,2,0:T(8,128)(2,1)S(1)} all-to-all(bf16[16,128,256]{1,2,0:T(8,128)(2,1)S(1)} %stack.2), channel_id=1, replica_groups=mesh['ctx'=16,'heads'=16] {'heads'}, dimensions={0} | all-to-all | bytes 2097152 | tf_op jit(solution)/shard_map/all_to_all | solution.py:66
  108.8 0.3 reduce_sum.52
  109.1 0.5 fusion.17
  109.6 2.4 %fusion.6 = bf16[128,512]{1,0:T(8,128)(2,1)} fusion(f32[128,512]{1,0:T(8,128)S(1)} %fusion.17, bf16[128,1024]{0,1:T(8,128)(2,1)S(1)} %bitcast.42, bf16[512,1024]{1,0:T(8,128)(2,1)} %param.16), kind=kOutput, calls=%fused_computation.16 | convolution fusion | flops 134348800 | bytes 1703936 | tf_op jit(solution)/shard_map/dot_general | solution.py:79
  112.3 0.2 select_reduce_fusion
  112.7 59.5 %all-gather.2.cloned.1.call-done = bf16[128,8192]{1,0:T(8,128)(2,1)} async-done(((bf16[128,512]{1,0:T(8,128)(2,1)}), bf16[128,8192]{1,0:T(8,128)(2,1)}) %all-gather.2.cloned.1.call-update) | async-done | bytes 2097168 | tf_op jit(solution)/shard_map/all_gather | solution.py:84
  172.1 6.1 %convolution_convert_fusion = bf16[128,480]{0,1:T(8,128)(2,1)S(1)} fusion(bf16[128,8192]{1,0:T(8,128)(2,1)} %all-gather.2.cloned.1.call-done, bf16[480,8192]{1,0:T(8,128)(2,1)} %param.17), kind=kOutput, calls=%fused_computation.17 | convolution fusion | flops 1006694400 | bytes 10084352 | tf_op jit(solution)/shard_map/dot_general | solution.py:83
  178.3 1.6 broadcast_select_fusion
  179.9 5.6 %all-to-all-start.3 = ((bf16[16,2,64,480]{3,2,1,0:T(8,128)(2,1)}), bf16[16,2,64,480]{3,2,1,0:T(8,128)(2,1)}, u32[]{:S(2)}, u32[]{:S(2)}) async-start(bf16[16,2,64,480]{3,2,1,0:T(8,128)(2,1)} %broadcast_select_fusion), calls=%async_computation.3 | async-start | bytes 4194304 | tf_op jit(solution)/shard_map/all_to_all | solution.py:153
  185.6 0.2 dynamic-slice_reduce_fusion.1
  186.2 3.5 %fusion.5 = bf16[1024,128]{1,0:T(8,128)(2,1)S(1)} fusion(bf16[2048,1024]{1,0:T(8,128)(2,1)} %copy-done.1, bf16[2048,256]{1,0:T(8,128)(2,1)S(1)} %bitcast.40), kind=kOutput, calls=%fused_computation.14 | convolution fusion | flops 537133056 | bytes 4980736 | tf_op jit(solution)/shard_map/dot_general | solution.py:129
  189.7 0.9 reshape.186
  190.6 24.5 %all-to-all-done.3 = bf16[16,2,64,480]{3,2,1,0:T(8,128)(2,1)} async-done(((bf16[16,2,64,480]{3,2,1,0:T(8,128)(2,1)}), bf16[16,2,64,480]{3,2,1,0:T(8,128)(2,1)}, u32[]{:S(2)}, u32[]{:S(2)}) %all-to-all-start.3) | async-done | bytes 1966112 | tf_op jit(solution)/shard_map/all_to_all | solution.py:153
  215.1 2.2 gather_fusion
  217.4 0.8 copy.38
  (37 shorter events, 1.4 us)
Async XLA Ops:
  7.2 101.9 %copy-start = (bf16[512,1024]{1,0:T(8,128)(2,1)S(1)}, bf16[512,1024]{1,0:T(8,128)(2,1)}, u32[]{:S(2)}) copy-start(bf16[512,1024]{1,0:T(8,128)(2,1)} %param.15) | copy-start | bytes 3145732
  9.2 21.4 %all-to-all-start = ((bf16[16,128,256]{2,1,0:T(8,128)(2,1)}), bf16[16,128,256]{2,1,0:T(8,128)(2,1)S(1)}, u32[]{:S(2)}, u32[]{:S(2)}) async-start(bf16[16,128,256]{2,1,0:T(8,128)(2,1)} %broadcast_in_dim.90), calls=%async_computation | async-start | bytes 2097152 | tf_op jit(solution)/shard_map/all_to_all | solution.py:16
  15.5 156.6 %all-gather.2.cloned.1.call-start = ((), (), s32[]{:S(2)}) async-start(), calls=%async_computation.4 | async-start | bytes 2228224 | tf_op jit(solution)/shard_map/all_gather | solution.py:84
  30.6 4.4 %copy-start.2 = (bf16[16,128,256]{2,1,0:T(8,128)(2,1)}, bf16[16,128,256]{2,1,0:T(8,128)(2,1)S(1)}, u32[]{:S(2)}) copy-start(bf16[16,128,256]{2,1,0:T(8,128)(2,1)S(1)} %all-to-all-done) | copy-start | bytes 3145732
  37.2 1.9 copy-start.1
  40.9 71.1 %copy-start.4 = (s32[16]{0:T(128)S(1)}, s32[16]{0:T(128)}, u32[]{:S(2)}) copy-start(s32[16]{0:T(128)} %param.19) | copy-start | bytes 196
  40.9 71.4 %copy-start.5 = (s32[32]{0:T(128)S(1)}, s32[32]{0:T(128)}, u32[]{:S(2)}) copy-start(s32[32]{0:T(128)} %param.18) | copy-start | bytes 388
  112.7 73.5 %copy-start.3 = (bf16[16,128,256]{2,1,0:T(8,128)(2,1)S(1)}, bf16[16,128,256]{2,1,0:T(8,128)(2,1)}, u32[]{:S(2)}) copy-start(bf16[16,128,256]{2,1,0:T(8,128)(2,1)} %copy-done.2) | copy-start | bytes 3145732
  179.9 35.2 %all-to-all-start.3 = ((bf16[16,2,64,480]{3,2,1,0:T(8,128)(2,1)}), bf16[16,2,64,480]{3,2,1,0:T(8,128)(2,1)}, u32[]{:S(2)}, u32[]{:S(2)}) async-start(bf16[16,2,64,480]{3,2,1,0:T(8,128)(2,1)} %broadcast_select_fusion), calls=%async_computation.3 | async-start | bytes 4194304 | tf_op jit(solution)/shard_map/all_to_all | solution.py:153
Sparse Core Ops, SparseCore 0:
  112.1 59.9 all-gather.1
